TPU v7x, 256 devices: a whole 4x4x8 slice. The times are simulated.
256 devices in a mesh: row: 16 (over x_hi, z), col: 16 (over x_lo, y, core).
Axes of the slice: x: 4 (x_hi: 2, x_lo: 2; x = x_hi * 2 + x_lo), y: 4, z: 8, core: 2. Of those that a mesh axis runs over, the one named last changes fastest.
Arguments:
- log_rate: float32 [1048576], P(('row', 'col')), may hold values from -0.5 to 1
- state: float32 [1048576], P(('row', 'col')), may hold values from 0.2 to 1
- excess: float32 [1048576], P(('row', 'col')), may hold values from -0.3 to 0.3
- normal_stress: float32 [1048576], P(('row', 'col')), may hold values from 2 to 4
- rate_param: float32 [1048576], P(('row', 'col')), may hold values from 0.5 to 1
- state_param: float32 [1048576], P(('row', 'col')), may hold values from 0.5 to 1.5
- slip_length: float32 [1048576], P(('row', 'col')), may hold values from 1 to 4
- self_stiffness: float32 [1048576], P(('row', 'col')), may hold values from 0.2 to 1
- damping: float32 [1048576], P(('row', 'col')), may hold values from 1 to 2
- blocks: bfloat16 [16, 16, 512, 4096], P('row', 'col'), may hold values from -0.1796875 to 0.1796875
- pattern: int32 [16, 16, 512, 2], P('row', 'col'), may hold values from 0 to 1023
- counts: int32 [16, 16], P('row', 'col'), may hold values from 1 to 512, as said below
Outputs:
- final_log_rate: float32 [1048576], P(('row', 'col'))
- final_state: float32 [1048576], P(('row', 'col'))
- final_stress: float32 [1048576], P(('row', 'col'))
Inputs may be any that keep to these rules, and one draw needn't show every extreme that they name: `counts`: every device holds at least one live tile; some device of the first index of row holds 512.
All inputs are finite; a program needn't handle non-finite values.
Results may differ from a plain program's by a relative error of at most 0.0014.
Values may be sent and summed in bfloat16 or wider, within the bound.
No kernel may reach another device: no remote copies, remote signals or barrier semaphores. Data moves between devices by JAX's collectives and lax.ppermute only.
A program may use at most 64 MiB of HBM per device.

v0:
```python
import math
import jax
import jax.numpy as jnp
from jax import lax
from jax.sharding import PartitionSpec as P

STEPS = 2
NEWTON = 4
time_step = 0.25


def inverse_sinh(value):
    return jnp.log(value + jnp.sqrt(1.0 + value * value))


def sweep(
    kernel_tiles,
    places,
    first_slot,
    limit_slot,
    row_rates,
    col_rates,
    owner_row,
    my_col,
    per_seg,
    row_total,
    col_total,
):
    slab_length = kernel_tiles.shape[0]
    group_size = math.gcd(128, slab_length)
    row_pieces = row_rates.reshape(-1, 64)
    col_pieces = col_rates.reshape(-1, 64)

    def turn_body(turn_index, totals):
        row_acc, col_acc = totals
        begin_slot = turn_index * group_size
        block_tiles = lax.dynamic_slice_in_dim(kernel_tiles, begin_slot, group_size, 0).reshape(
            group_size, 64, 64
        )
        block_places = lax.dynamic_slice_in_dim(places, begin_slot, group_size, 0)
        row_slot = block_places[:, 0]
        col_slot = block_places[:, 1]
        slot_ids = begin_slot + jnp.arange(group_size, dtype=jnp.int32)
        active = (slot_ids >= first_slot) & (slot_ids < limit_slot)
        diagonal = (col_slot // per_seg == owner_row) & (
            row_slot == my_col * per_seg + col_slot % per_seg
        )
        direct = jnp.einsum(
            "bij,bj->bi", block_tiles, col_pieces[col_slot], preferred_element_type=jnp.float32
        )
        mirror = jnp.einsum(
            "bij,bi->bj", block_tiles, row_pieces[row_slot], preferred_element_type=jnp.float32
        )
        direct = jnp.where(active[:, None], direct, 0.0)
        mirror = jnp.where((active & jnp.logical_not(diagonal))[:, None], mirror, 0.0)
        return (row_acc.at[row_slot].add(direct), col_acc.at[col_slot].add(mirror))

    lower = jnp.maximum(first_slot, 0) // group_size
    upper = (jnp.maximum(limit_slot, 0) + group_size - 1) // group_size
    upper = jnp.maximum(upper, lower)
    return lax.fori_loop(lower, upper, turn_body, (row_total, col_total))


def friction_solve(rate_log, stress, state, normal_stress, rate_param, damping):
    for turn_index in range(NEWTON):
        speed = jnp.exp(rate_log)
        ratio = 0.5 * jnp.exp(rate_log + state / rate_param)
        misfit = stress - damping * speed - normal_stress * rate_param * inverse_sinh(ratio)
        slope = -damping * speed - normal_stress * rate_param * ratio / jnp.sqrt(
            1.0 + ratio * ratio
        )
        rate_log = rate_log - misfit / slope
    return rate_log


def on_device(
    log_rate,
    state,
    excess,
    normal_stress,
    rate_param,
    state_param,
    slip_length,
    self_stiffness,
    damping,
    blocks,
    pattern,
    counts,
):
    patches = log_rate.shape[0]
    per_seg = patches // 64
    my_row = lax.axis_index("row")
    my_col = lax.axis_index("col")
    row_count = lax.axis_size("row")
    col_count = lax.axis_size("col")
    kernel_tiles = blocks.reshape(blocks.shape[2], blocks.shape[3])
    places = pattern.reshape(pattern.shape[2], 2)
    stored = counts[0, 0]
    rate_log = log_rate
    balance = normal_stress * rate_param * inverse_sinh(
        0.5 * jnp.exp(log_rate + state / rate_param)
    ) + damping * jnp.exp(log_rate)
    stress = balance * (1.0 + excess)
    for step_index in range(STEPS):
        speed = jnp.exp(rate_log)
        pushed = (speed - 1.0).astype(jnp.bfloat16)
        row_rates = lax.all_gather(pushed, "col", axis=0, tiled=True)
        col_rates = lax.all_gather(pushed, "row", axis=0, tiled=True)
        row_total = jnp.zeros((col_count * per_seg, 64), jnp.float32)
        col_total = jnp.zeros((row_count * per_seg, 64), jnp.float32)
        row_total, col_total = sweep(
            kernel_tiles,
            places,
            0,
            stored,
            row_rates,
            col_rates,
            my_row,
            my_col,
            per_seg,
            row_total,
            col_total,
        )
        stress_rate = lax.psum_scatter(
            row_total.reshape(-1).astype(jnp.bfloat16), "col", scatter_dimension=0, tiled=True
        ).astype(jnp.float32) + lax.psum_scatter(
            col_total.reshape(-1).astype(jnp.bfloat16), "row", scatter_dimension=0, tiled=True
        ).astype(
            jnp.float32
        )
        new_stress = stress + time_step * (stress_rate - self_stiffness * (speed - 1.0))
        state = state + time_step * (state_param / slip_length) * (
            jnp.exp(-state / state_param) - speed
        )
        stress = new_stress
        rate_log = friction_solve(rate_log, stress, state, normal_stress, rate_param, damping)
    return (rate_log, state, stress)


def solution(mesh):
    in_specs = (
        P(("row", "col")),
        P(("row", "col")),
        P(("row", "col")),
        P(("row", "col")),
        P(("row", "col")),
        P(("row", "col")),
        P(("row", "col")),
        P(("row", "col")),
        P(("row", "col")),
        P("row", "col", None, None),
        P("row", "col", None, None),
        P("row", "col"),
    )
    out_specs = (P(("row", "col")), P(("row", "col")), P(("row", "col")))
    return jax.shard_map(
        on_device, mesh=mesh, in_specs=in_specs, out_specs=out_specs, check_vma=False
    )
```

profile of v0, /device:TPU:1, one launch (start us, length us, event | category | flops | bytes accessed | tf_op | source)
XLA Modules:
  0.0 812.9 jit_solution(1112874415453995245)
XLA Ops:
  8.6 38.1 %all_gather.12 = bf16[65536]{0:T(1024)(128)(2,1)S(1)} all-gather(bf16[4096]{0:T(1024)(128)(2,1)S(1)} %add_convert_fusion), channel_id=1, replica_groups=mesh['row'=16,'col'=16] {'row'}, dimensions={0}, use_global_device_ids=true | all-gather | bytes 139264 | tf_op jit(solution)/shard_map/all_gather | solution.py:108
  46.7 27.0 %all_gather.13 = bf16[65536]{0:T(1024)(128)(2,1)S(1)} all-gather(bf16[4096]{0:T(1024)(128)(2,1)S(1)} %add_convert_fusion), channel_id=1, replica_groups=mesh['row'=16,'col'=16] {'col'}, dimensions={0}, use_global_device_ids=true | all-gather | bytes 139264 | tf_op jit(solution)/shard_map/all_gather | solution.py:107
  73.7 6.5 copy.16
  82.9 42.3 %while.28 = (s32[]{:T(128)}, f32[1024,64]{1,0:T(8,128)}, f32[1024,64]{1,0:T(8,128)}, s32[]{:T(128)}, s32[512,2]{0,1:T(2,128)S(1)}, /*index=5*/s32[]{:T(128)}, bf...) while((s32[]{:T(128)}, f32[1024,64]{1,0:T(8,128)}, ...), condition=%wide.region_3.4_spmd, body=%wide.region_0.3_spmd.sunk | while | flops 2136966 | bytes 9749571 | solution.py:61
  82.9 1.3 constant_dynamic-slice_fusion.9
  84.2 3.5 copy.45
  89.8 1.5 scatter_custom_fusion.18
  92.1 1.2 fusion.80
  93.9 3.1 scatter_custom_fusion.19
  97.0 1.3 constant_dynamic-slice_fusion.9
  98.3 3.5 copy.45
  103.9 1.5 scatter_custom_fusion.18
  106.2 1.2 fusion.80
  108.0 3.1 scatter_custom_fusion.19
  111.1 1.3 constant_dynamic-slice_fusion.9
  112.4 3.5 copy.45
  118.0 1.5 scatter_custom_fusion.18
  120.3 1.2 fusion.80
  122.1 3.1 scatter_custom_fusion.19
  125.3 1.1 convert_element_type.46
  127.3 1.1 convert_element_type.43
  131.8 147.2 %all-reduce.11.cloned.1.call-done = bf16[65536]{0:T(1024)(128)(2,1)} async-done(((bf16[65536]{0:T(1024)(128)(2,1)}), bf16[65536]{0:T(1024)(128)(2,1)}) %all-reduce.11.cloned.1.call-update) | async-done | bytes 131088
  278.9 133.4 %all-reduce.9.cloned.1.call-done = bf16[65536]{0:T(1024)(128)(2,1)} async-done(((bf16[65536]{0:T(1024)(128)(2,1)}), bf16[65536]{0:T(1024)(128)(2,1)}) %all-reduce.9.cloned.1.call-update) | async-done | bytes 131088
  412.4 1.5 fusion.48
  413.9 34.4 %all_gather.14 = bf16[65536]{0:T(1024)(128)(2,1)S(1)} all-gather(bf16[4096]{0:T(1024)(128)(2,1)S(1)} %get-tuple-element.346), channel_id=1, replica_groups=mesh['row'=16,'col'=16] {'row'}, dimensions={0}, use_global_device_ids=true | all-gather | bytes 139264 | tf_op jit(solution)/shard_map/all_gather | solution.py:108
  448.3 24.1 %all_gather.15 = bf16[65536]{0:T(1024)(128)(2,1)S(1)} all-gather(bf16[4096]{0:T(1024)(128)(2,1)S(1)} %get-tuple-element.346), channel_id=1, replica_groups=mesh['row'=16,'col'=16] {'col'}, dimensions={0}, use_global_device_ids=true | all-gather | bytes 139264 | tf_op jit(solution)/shard_map/all_gather | solution.py:107
  472.5 0.9 reshape.85
  475.0 42.3 %while.29 = (s32[]{:T(128)}, f32[1024,64]{1,0:T(8,128)}, f32[1024,64]{1,0:T(8,128)}, s32[]{:T(128)}, s32[512,2]{0,1:T(2,128)S(1)}, /*index=5*/s32[]{:T(128)}, bf...) while((s32[]{:T(128)}, f32[1024,64]{1,0:T(8,128)}, ...), condition=%wide.region_9.10_spmd, body=%wide.region_6.9_spmd.sunk | while | flops 2136966 | bytes 9749571 | solution.py:61
  475.0 1.3 constant_dynamic-slice_fusion.11
  476.3 3.5 copy.48
  481.9 1.5 scatter_custom_fusion.22
  484.2 1.2 fusion.89
  486.0 3.1 scatter_custom_fusion.23
  489.1 1.3 constant_dynamic-slice_fusion.11
  490.4 3.5 copy.48
  496.0 1.5 scatter_custom_fusion.22
  498.3 1.2 fusion.89
  500.1 3.1 scatter_custom_fusion.23
  503.2 1.3 constant_dynamic-slice_fusion.11
  504.5 3.5 copy.48
  510.1 1.5 scatter_custom_fusion.22
  512.4 1.2 fusion.89
  514.2 3.1 scatter_custom_fusion.23
  517.3 1.1 convert_element_type.53
  519.3 1.1 convert_element_type.50
  521.2 150.4 %all-reduce.15.cloned.1.call-done = bf16[65536]{0:T(1024)(128)(2,1)} async-done(((bf16[65536]{0:T(1024)(128)(2,1)}), bf16[65536]{0:T(1024)(128)(2,1)}) %all-reduce.15.cloned.1.call-update) | async-done | bytes 131088
  671.6 133.2 %all-reduce.13.cloned.1.call-done = bf16[65536]{0:T(1024)(128)(2,1)} async-done(((bf16[65536]{0:T(1024)(128)(2,1)}), bf16[65536]{0:T(1024)(128)(2,1)}) %all-reduce.13.cloned.1.call-update) | async-done | bytes 131088
  804.8 1.5 divide_subtract_fusion
  (134 shorter events, 30.6 us)
Async XLA Ops:
  7.2 271.8 %all-reduce.11.cloned.1.call-start = ((), (), s32[]{:S(2)}) async-start(), calls=%async_computation.1 | async-start | bytes 262144
  73.7 9.2 %copy-start.16 = (s32[1,1,512,2]{2,3,1,0:T(2,128)S(1)}, s32[1,1,512,2]{2,3,1,0:T(2,128)}, u32[]{:S(2)}) copy-start(s32[1,1,512,2]{2,3,1,0:T(2,128)} %param.26) | copy-start | bytes 12292
  87.7 2.1 copy-start.2
  87.7 3.6 copy-start.1
  91.3 5.7 copy-start.3
  101.8 2.1 copy-start.2
  101.8 3.6 copy-start.1
  105.4 5.7 copy-start.3
  115.9 2.1 copy-start.2
  115.9 3.6 copy-start.1
  119.5 5.7 copy-start.3
  125.2 4.1 copy-start.19
  125.2 4.7 copy-start.18
  125.2 287.1 %copy-start.6 = (f32[4096]{0:T(1024)S(1)}, f32[4096]{0:T(1024)}, u32[]{:S(2)}) copy-start(f32[4096]{0:T(1024)} %param.16) | copy-start | bytes 49156
  125.2 287.1 %copy-start.7 = (f32[4096]{0:T(1024)S(1)}, f32[4096]{0:T(1024)}, u32[]{:S(2)}) copy-start(f32[4096]{0:T(1024)} %param.24) | copy-start | bytes 49156
  125.2 287.1 %copy-start.8 = (f32[4096]{0:T(1024)S(1)}, f32[4096]{0:T(1024)}, u32[]{:S(2)}) copy-start(f32[4096]{0:T(1024)} %param.20) | copy-start | bytes 49156
  125.2 287.1 %copy-start.9 = (f32[4096]{0:T(1024)S(1)}, f32[4096]{0:T(1024)}, u32[]{:S(2)}) copy-start(f32[4096]{0:T(1024)} %param.17) | copy-start | bytes 49156
  125.2 287.1 %copy-start.10 = (f32[4096]{0:T(1024)S(1)}, f32[4096]{0:T(1024)}, u32[]{:S(2)}) copy-start(f32[4096]{0:T(1024)} %param.21) | copy-start | bytes 49156
  125.3 287.1 %copy-start.11 = (f32[4096]{0:T(1024)S(1)}, f32[4096]{0:T(1024)}, u32[]{:S(2)}) copy-start(f32[4096]{0:T(1024)} %param.22) | copy-start | bytes 49156
  125.3 287.1 %copy-start.12 = (f32[4096]{0:T(1024)S(1)}, f32[4096]{0:T(1024)}, u32[]{:S(2)}) copy-start(f32[4096]{0:T(1024)} %param.23) | copy-start | bytes 49156
  125.3 287.1 %copy-start.13 = (f32[4096]{0:T(1024)S(1)}, f32[4096]{0:T(1024)}, u32[]{:S(2)}) copy-start(f32[4096]{0:T(1024)} %param.18) | copy-start | bytes 49156
  125.3 287.1 %copy-start.17 = (f32[4096]{0:T(1024)S(1)}, f32[4096]{0:T(1024)}, u32[]{:S(2)}) copy-start(f32[4096]{0:T(1024)} %param.19) | copy-start | bytes 49156
  127.3 285.0 %all-reduce.9.cloned.1.call-start = ((), (), s32[]{:S(2)}) async-start(), calls=%async_computation | async-start | bytes 262144
  129.2 542.3 %all-reduce.15.cloned.1.call-start = ((), (), s32[]{:S(2)}) async-start(), calls=%async_computation.3 | async-start | bytes 262144
  479.8 2.1 copy-start.4
  479.8 3.6 copy-start
  483.5 5.7 copy-start.5
  493.9 2.1 copy-start.4
  493.9 3.6 copy-start
  497.6 5.7 copy-start.5
  508.0 2.1 copy-start.4
  508.0 3.6 copy-start
  511.7 5.7 copy-start.5
  517.3 287.5 %copy-start.14 = (f32[4096]{0:T(1024)S(1)}, f32[4096]{0:T(1024)}, u32[]{:S(2)}) copy-start(f32[4096]{0:T(1024)} %get-tuple-element.347) | copy-start | bytes 49156
  517.3 287.5 %copy-start.15 = (f32[4096]{0:T(1024)S(1)}, f32[4096]{0:T(1024)}, u32[]{:S(2)}) copy-start(f32[4096]{0:T(1024)} %get-tuple-element.348) | copy-start | bytes 49156
  519.2 285.6 %all-reduce.13.cloned.1.call-start = ((), (), s32[]{:S(2)}) async-start(), calls=%async_computation.2 | async-start | bytes 262144
Sparse Core Ops, SparseCore 0:
  127.4 151.4 all-reduce.10
  281.5 130.7 all-reduce.8
  519.4 152.1 all-reduce.14
  674.0 130.7 all-reduce.12
where the time goes:
time: 814 us; the launch traced here: 813 us
  waiting for transfers between devices  564 us (69%)
  blocking collectives  124 us (15%)
  local copies, waits for them, and re-layouts  53.7 us (7%)
  other arithmetic  43.9 us (5%)
  between operations  15.9 us (2%)
  matrix products  10.9 us (1%)
    unnamed x8, waiting for transfers between devices  564 us
    all_gather x2, blocking collectives, on_device(): col_rates = lax.all_gather(pushed, 'row', axis=0, tiled=True)  72.5 us
    all_gather x2, blocking collectives, on_device(): row_rates = lax.all_gather(pushed, 'col', axis=0, tiled=True)  51.1 us
    scatter-add x12, other arithmetic, turn_body(): return (row_acc.at[row_slot].add(direct), col_acc.at[col_slot].add(mirror))  27.6 us
    reshape x6, local copies, waits for them, and re-layouts, turn_body(): lax.dynamic_slice_in_dim(kernel_tiles, begin_slot, group_size, 0)  21 us
  transfers between devices with their start and end apart: 4, of which 4 were waited for; matrix products, arithmetic and copies ran while one was open for 1% of the time, Pallas kernels for 0%

commit v1 on v0

--- a/solution.py
+++ b/solution.py
@@ -105,7 +105,9 @@
         speed = jnp.exp(rate_log)
         pushed = (speed - 1.0).astype(jnp.bfloat16)
         row_rates = lax.all_gather(pushed, "col", axis=0, tiled=True)
-        col_rates = lax.all_gather(pushed, "row", axis=0, tiled=True)
+        col_rates = jnp.concatenate(
+            lax.all_to_all(jnp.stack([pushed] * lax.axis_size("row")), "row", 0, 0), axis=0
+        )
         row_total = jnp.zeros((col_count * per_seg, 64), jnp.float32)
         col_total = jnp.zeros((row_count * per_seg, 64), jnp.float32)
         row_total, col_total = sweep(

time: 814 us -> 764 us (0.939)
  blocking collectives: 124 us -> 37.4 us
  starting transfers between devices: 0.16 us -> 20.7 us
  local copies, waits for them, and re-layouts: 53.7 us -> 67.1 us
    all_gather x2 -> x0, blocking collectives: 72.5 us -> none  [on_device(): col_rates = lax.all_gather(pushed, 'row', axis=0, tiled=True)]
    all_to_all x0 -> x2, starting transfers between devices: none -> 20.5 us  [on_device(): lax.all_to_all(jnp.stack([pushed] * lax.axis_size('row')), 'row', 0, 0)]
    all_gather x2, blocking collectives: 51.1 us -> 37.4 us  [on_device(): row_rates = lax.all_gather(pushed, 'col', axis=0, tiled=True)]
    scatter-add x12, other arithmetic: 27.6 us -> 18.5 us  [turn_body(): return (row_acc.at[row_slot].add(direct), col_acc.at[col_slot].add(mirror))]
  transfers between devices with their start and end apart: 4 -> 6, of which waited for: 4 -> 4; matrix products, arithmetic and copies ran while one was open for 1% -> 2% of each run, Pallas kernels for 0% -> 0%
where the time goes in v1:
time: 764 us; the launch traced here: 763 us
  waiting for transfers between devices  571 us (75%)
  local copies, waits for them, and re-layouts  67.1 us (9%)
  other arithmetic  39.2 us (5%)
  blocking collectives  37.4 us (5%)
  starting transfers between devices  20.7 us (3%)
  between operations  16.1 us (2%)
  matrix products  10.9 us (1%)
    unnamed x8, waiting for transfers between devices  571 us
    all_gather x2, blocking collectives, on_device(): row_rates = lax.all_gather(pushed, 'col', axis=0, tiled=True)  37.4 us
    reshape x6, local copies, waits for them, and re-layouts, turn_body(): lax.dynamic_slice_in_dim(kernel_tiles, begin_slot, group_size, 0)  21 us
    all_to_all x2, starting transfers between devices, on_device(): lax.all_to_all(jnp.stack([pushed] * lax.axis_size('row')), 'row', 0, 0)  20.5 us
    scatter-add x12, other arithmetic, turn_body(): return (row_acc.at[row_slot].add(direct), col_acc.at[col_slot].add(mirror))  18.5 us
  transfers between devices with their start and end apart: 6, of which 4 were waited for; matrix products, arithmetic and copies ran while one was open for 2% of the time, Pallas kernels for 0%

profile of v1, /device:TPU:1, one launch (start us, length us, event | category | flops | bytes accessed | tf_op | source)
XLA Modules:
  0.0 762.6 jit_solution(7761970742180390504)
XLA Ops:
  8.6 1.3 reduce.2
  10.6 11.6 %all-to-all-start = ((bf16[16,2,2048]{2,1,0:T(2,128)(2,1)}), bf16[16,2,2048]{2,1,0:T(2,128)(2,1)S(1)}, u32[]{:S(2)}, u32[]{:S(2)}) async-start(bf16[16,2,2048]{2,1,0:T(2,128)(2,1)} %reshape.180), calls=%async_computation | async-start | bytes 262144 | tf_op jit(solution)/shard_map/all_to_all | solution.py:109
  22.9 6.5 copy.16
  29.4 20.2 %all_gather.6 = bf16[65536]{0:T(1024)(128)(2,1)S(1)} all-gather(bf16[4096]{0:T(1024)(128)(2,1)S(1)} %add_convert_fusion), channel_id=1, replica_groups=mesh['row'=16,'col'=16] {'col'}, dimensions={0}, use_global_device_ids=true | all-gather | bytes 139264 | tf_op jit(solution)/shard_map/all_gather | solution.py:107
  53.3 43.2 %while.28 = (s32[]{:T(128)}, f32[1024,64]{1,0:T(8,128)}, f32[1024,64]{1,0:T(8,128)}, s32[]{:T(128)}, s32[512,2]{0,1:T(2,128)S(1)}, /*index=5*/s32[]{:T(128)}, bf...) while((s32[]{:T(128)}, f32[1024,64]{1,0:T(8,128)}, ...), condition=%wide.region_3.4_spmd, body=%wide.region_0.3_spmd.sunk | while | flops 2136966 | bytes 11321955 | solution.py:61
  53.3 1.3 constant_dynamic-slice_fusion.9
  54.6 3.5 copy.45
  58.2 1.7 gather_fusion
  61.2 1.5 scatter_custom_fusion.18
  65.4 1.5 scatter_custom_fusion.19
  67.7 1.3 constant_dynamic-slice_fusion.9
  69.0 3.5 copy.45
  72.6 1.7 gather_fusion
  75.6 1.5 scatter_custom_fusion.18
  77.9 1.2 fusion.80
  79.8 1.5 scatter_custom_fusion.19
  82.1 1.3 constant_dynamic-slice_fusion.9
  83.4 3.5 copy.45
  87.0 1.7 gather_fusion
  90.0 1.5 scatter_custom_fusion.18
  92.3 1.2 fusion.80
  94.2 1.5 scatter_custom_fusion.19
  103.0 150.2 %all-reduce.11.cloned.1.call-done = bf16[65536]{0:T(1024)(128)(2,1)} async-done(((bf16[65536]{0:T(1024)(128)(2,1)}), bf16[65536]{0:T(1024)(128)(2,1)}) %all-reduce.11.cloned.1.call-update) | async-done | bytes 131088
  253.2 133.4 %all-reduce.9.cloned.1.call-done = bf16[65536]{0:T(1024)(128)(2,1)} async-done(((bf16[65536]{0:T(1024)(128)(2,1)}), bf16[65536]{0:T(1024)(128)(2,1)}) %all-reduce.9.cloned.1.call-update) | async-done | bytes 131088
  386.7 1.5 fusion.48
  388.4 1.3 reduce.3
  390.4 9.0 %all-to-all-start.1 = ((bf16[16,2,2048]{2,1,0:T(2,128)(2,1)}), bf16[16,2,2048]{2,1,0:T(2,128)(2,1)S(1)}, u32[]{:S(2)}, u32[]{:S(2)}) async-start(bf16[16,2,2048]{2,1,0:T(2,128)(2,1)} %reshape.182), calls=%async_computation.1 | async-start | bytes 262144 | tf_op jit(solution)/shard_map/all_to_all | solution.py:109
  399.4 17.1 %all_gather.7 = bf16[65536]{0:T(1024)(128)(2,1)S(1)} all-gather(bf16[4096]{0:T(1024)(128)(2,1)S(1)} %get-tuple-element.346), channel_id=1, replica_groups=mesh['row'=16,'col'=16] {'col'}, dimensions={0}, use_global_device_ids=true | all-gather | bytes 139264 | tf_op jit(solution)/shard_map/all_gather | solution.py:107
  420.2 43.2 %while.29 = (s32[]{:T(128)}, f32[1024,64]{1,0:T(8,128)}, f32[1024,64]{1,0:T(8,128)}, s32[]{:T(128)}, s32[512,2]{0,1:T(2,128)S(1)}, /*index=5*/s32[]{:T(128)}, bf...) while((s32[]{:T(128)}, f32[1024,64]{1,0:T(8,128)}, ...), condition=%wide.region_9.10_spmd, body=%wide.region_6.9_spmd.sunk | while | flops 2136966 | bytes 11321955 | solution.py:61
  420.2 1.3 constant_dynamic-slice_fusion.11
  421.5 3.5 copy.48
  425.1 1.7 gather_fusion.2
  428.1 1.5 scatter_custom_fusion.22
  432.3 1.5 scatter_custom_fusion.23
  434.7 1.3 constant_dynamic-slice_fusion.11
  435.9 3.5 copy.48
  439.5 1.7 gather_fusion.2
  442.6 1.5 scatter_custom_fusion.22
  446.7 1.5 scatter_custom_fusion.23
  449.1 1.3 constant_dynamic-slice_fusion.11
  450.4 3.5 copy.48
  453.9 1.7 gather_fusion.2
  457.0 1.5 scatter_custom_fusion.22
  459.2 1.2 fusion.89
  461.1 1.5 scatter_custom_fusion.23
  467.4 153.8 %all-reduce.15.cloned.1.call-done = bf16[65536]{0:T(1024)(128)(2,1)} async-done(((bf16[65536]{0:T(1024)(128)(2,1)}), bf16[65536]{0:T(1024)(128)(2,1)}) %all-reduce.15.cloned.1.call-update) | async-done | bytes 131088
  621.3 133.2 %all-reduce.13.cloned.1.call-done = bf16[65536]{0:T(1024)(128)(2,1)} async-done(((bf16[65536]{0:T(1024)(128)(2,1)}), bf16[65536]{0:T(1024)(128)(2,1)}) %all-reduce.13.cloned.1.call-update) | async-done | bytes 131088
  754.5 1.5 divide_subtract_fusion
  (171 shorter events, 44.5 us)
Async XLA Ops:
  10.6 39.2 %all-to-all-start = ((bf16[16,2,2048]{2,1,0:T(2,128)(2,1)}), bf16[16,2,2048]{2,1,0:T(2,128)(2,1)S(1)}, u32[]{:S(2)}, u32[]{:S(2)}) async-start(bf16[16,2,2048]{2,1,0:T(2,128)(2,1)} %reshape.180), calls=%async_computation | async-start | bytes 262144 | tf_op jit(solution)/shard_map/all_to_all | solution.py:109
  22.2 231.0 %all-reduce.11.cloned.1.call-start = ((), (), s32[]{:S(2)}) async-start(), calls=%async_computation.3 | async-start | bytes 262144
  29.4 23.9 %copy-start.24 = (s32[1,1,512,2]{2,3,1,0:T(2,128)S(1)}, s32[1,1,512,2]{2,3,1,0:T(2,128)}, u32[]{:S(2)}) copy-start(s32[1,1,512,2]{2,3,1,0:T(2,128)} %param.26) | copy-start | bytes 12292
  58.1 3.1 copy-start
  60.5 4.9 copy-start.2
  62.8 4.2 copy-start.1
  66.9 0.8 copy-start.3
  72.5 3.1 copy-start
  74.9 4.9 copy-start.2
  77.2 4.2 copy-start.1
  81.3 0.8 copy-start.3
  86.9 3.1 copy-start
  89.3 4.9 copy-start.2
  91.6 4.2 copy-start.1
  95.7 0.8 copy-start.3
  96.5 4.0 copy-start.27
  96.5 4.6 copy-start.26
  96.5 290.1 %copy-start.8 = (f32[4096]{0:T(1024)S(1)}, f32[4096]{0:T(1024)}, u32[]{:S(2)}) copy-start(f32[4096]{0:T(1024)} %param.16) | copy-start | bytes 49156
  96.5 290.1 %copy-start.9 = (f32[4096]{0:T(1024)S(1)}, f32[4096]{0:T(1024)}, u32[]{:S(2)}) copy-start(f32[4096]{0:T(1024)} %param.24) | copy-start | bytes 49156
  96.5 290.1 %copy-start.10 = (f32[4096]{0:T(1024)S(1)}, f32[4096]{0:T(1024)}, u32[]{:S(2)}) copy-start(f32[4096]{0:T(1024)} %param.20) | copy-start | bytes 49156
  96.6 290.1 %copy-start.12 = (f32[4096]{0:T(1024)S(1)}, f32[4096]{0:T(1024)}, u32[]{:S(2)}) copy-start(f32[4096]{0:T(1024)} %param.17) | copy-start | bytes 49156
  96.6 290.1 %copy-start.14 = (f32[4096]{0:T(1024)S(1)}, f32[4096]{0:T(1024)}, u32[]{:S(2)}) copy-start(f32[4096]{0:T(1024)} %param.21) | copy-start | bytes 49156
  96.6 290.1 %copy-start.16 = (f32[4096]{0:T(1024)S(1)}, f32[4096]{0:T(1024)}, u32[]{:S(2)}) copy-start(f32[4096]{0:T(1024)} %param.22) | copy-start | bytes 49156
  96.6 290.1 %copy-start.18 = (f32[4096]{0:T(1024)S(1)}, f32[4096]{0:T(1024)}, u32[]{:S(2)}) copy-start(f32[4096]{0:T(1024)} %param.23) | copy-start | bytes 49156
  96.6 290.0 %copy-start.20 = (f32[4096]{0:T(1024)S(1)}, f32[4096]{0:T(1024)}, u32[]{:S(2)}) copy-start(f32[4096]{0:T(1024)} %param.18) | copy-start | bytes 49156
  96.6 290.0 %copy-start.25 = (f32[4096]{0:T(1024)S(1)}, f32[4096]{0:T(1024)}, u32[]{:S(2)}) copy-start(f32[4096]{0:T(1024)} %param.19) | copy-start | bytes 49156
  98.6 288.0 %all-reduce.9.cloned.1.call-start = ((), (), s32[]{:S(2)}) async-start(), calls=%async_computation.2 | async-start | bytes 262144
  390.4 26.3 %all-to-all-start.1 = ((bf16[16,2,2048]{2,1,0:T(2,128)(2,1)}), bf16[16,2,2048]{2,1,0:T(2,128)(2,1)S(1)}, u32[]{:S(2)}, u32[]{:S(2)}) async-start(bf16[16,2,2048]{2,1,0:T(2,128)(2,1)} %reshape.182), calls=%async_computation.1 | async-start | bytes 262144 | tf_op jit(solution)/shard_map/all_to_all | solution.py:109
  399.4 221.9 %all-reduce.15.cloned.1.call-start = ((), (), s32[]{:S(2)}) async-start(), calls=%async_computation.5 | async-start | bytes 262144
  425.0 3.1 copy-start.4
  427.4 4.9 copy-start.6
  429.7 4.2 copy-start.5
  433.8 0.8 copy-start.7
  439.5 3.1 copy-start.4
  441.8 4.9 copy-start.6
  444.1 4.2 copy-start.5
  453.9 3.1 copy-start.4
  456.2 4.9 copy-start.6
  458.5 4.2 copy-start.5
  463.5 291.0 %copy-start.11 = (f32[4096]{0:T(1024)S(1)}, f32[4096]{0:T(1024)}, u32[]{:S(2)}) copy-start(f32[4096]{0:T(1024)} %param.20) | copy-start | bytes 49156
  463.5 291.0 %copy-start.13 = (f32[4096]{0:T(1024)S(1)}, f32[4096]{0:T(1024)}, u32[]{:S(2)}) copy-start(f32[4096]{0:T(1024)} %param.17) | copy-start | bytes 49156
  463.5 291.0 %copy-start.15 = (f32[4096]{0:T(1024)S(1)}, f32[4096]{0:T(1024)}, u32[]{:S(2)}) copy-start(f32[4096]{0:T(1024)} %param.21) | copy-start | bytes 49156
  463.5 291.0 %copy-start.17 = (f32[4096]{0:T(1024)S(1)}, f32[4096]{0:T(1024)}, u32[]{:S(2)}) copy-start(f32[4096]{0:T(1024)} %param.22) | copy-start | bytes 49156
  463.5 291.0 %copy-start.19 = (f32[4096]{0:T(1024)S(1)}, f32[4096]{0:T(1024)}, u32[]{:S(2)}) copy-start(f32[4096]{0:T(1024)} %param.23) | copy-start | bytes 49156
  463.5 291.0 %copy-start.21 = (f32[4096]{0:T(1024)S(1)}, f32[4096]{0:T(1024)}, u32[]{:S(2)}) copy-start(f32[4096]{0:T(1024)} %param.18) | copy-start | bytes 49156
  463.5 291.0 %copy-start.22 = (f32[4096]{0:T(1024)S(1)}, f32[4096]{0:T(1024)}, u32[]{:S(2)}) copy-start(f32[4096]{0:T(1024)} %get-tuple-element.347) | copy-start | bytes 49156
  463.5 291.0 %copy-start.23 = (f32[4096]{0:T(1024)S(1)}, f32[4096]{0:T(1024)}, u32[]{:S(2)}) copy-start(f32[4096]{0:T(1024)} %get-tuple-element.348) | copy-start | bytes 49156
  465.5 289.0 %all-reduce.13.cloned.1.call-start = ((), (), s32[]{:S(2)}) async-start(), calls=%async_computation.4 | async-start | bytes 262144
  (2 other events, 1.6 us)
Sparse Core Ops, SparseCore 0:
  98.7 154.4 all-reduce.10
  255.8 130.7 all-reduce.8
  465.6 155.6 all-reduce.14
  623.7 130.7 all-reduce.12
